TPU v7x, 512 devices: a whole 4x4x16 slice. The times are simulated.
512 devices in a mesh: blk: 128 (over z_lo, y, x), off: 4 (over z_hi, core).
Axes of the slice: x: 4, y: 4, z: 16 (z_hi: 2, z_lo: 8; z = z_hi * 8 + z_lo), core: 2. Of those that a mesh axis runs over, the one named last changes fastest.
Arguments:
- coefficients: bfloat16 [2048, 32, 128], P('blk', 'off'), may hold values from -12 to 12
Outputs:
- smoothed: float32 [2048, 32, 128], P(('blk', 'off'))
- log_degree: float32 [2048], P(('blk', 'off'))
All inputs are finite; a program needn't handle non-finite values.
Results may differ from a plain program's by a relative error of at most 0.005.
Values may be sent and summed in bfloat16 or wider, within the bound.
A program may use at most 64 MiB of HBM per device.

v0:
```python
import math
import jax
import jax.numpy as jnp
from jax import lax
from jax.sharding import PartitionSpec as P

epsilon = 1e-06
concentration = 40.0


def shifted(array, axis, by):
    count = lax.axis_size(axis)
    return lax.ppermute(array, axis, [(i, (i + by) % count) for i in range(count)])


def angle_tables(angular):
    half_width = angular // 2
    frequency = jnp.arange(half_width, dtype=jnp.int32)
    shifts = jnp.arange(angular, dtype=jnp.int32)
    product = frequency[:, None] * shifts[None, :] % angular
    phase = product.astype(jnp.float32) * (2.0 * math.pi / angular)
    forward = jnp.concatenate([jnp.cos(phase), -jnp.sin(phase)], axis=0)
    return (forward, forward.T)


def inverse_norms(block_values):
    values = block_values.astype(jnp.float32)
    return lax.rsqrt(jnp.sum(values * values, axis=(1, 2)) + epsilon)


def tile_terms(own_block, own_inverse, other_block, offset, forward, backward):
    row_count = own_block.shape[0]
    half_width = own_block.shape[2] // 2
    highest = lax.Precision.HIGHEST
    other_inverse = inverse_norms(other_block)
    swapped = jnp.concatenate(
        [other_block[:, :, half_width:], other_block[:, :, :half_width]], axis=2
    )
    direct = jnp.einsum("irc,jrc->ijc", own_block, other_block, preferred_element_type=jnp.float32)
    mixed_terms = jnp.einsum("irc,jrc->ijc", own_block, swapped, preferred_element_type=jnp.float32)
    real_part = direct[:, :, :half_width] + direct[:, :, half_width:]
    imag_part = mixed_terms[:, :, half_width:] - mixed_terms[:, :, :half_width]
    cross_spectrum = jnp.concatenate([real_part, imag_part], axis=2).reshape(
        row_count * row_count, -1
    )
    correlation = jnp.dot(
        cross_spectrum, forward, precision=highest, preferred_element_type=jnp.float32
    )
    correlation = correlation.reshape(row_count, row_count, -1)
    cosine = correlation * own_inverse[:, None, None] * other_inverse[None, :, None]
    same_image = jnp.arange(row_count)[:, None] == jnp.arange(row_count)[None, :]
    keep_mask = jnp.where(jnp.logical_and(offset == 0, same_image), 0.0, 1.0).astype(jnp.float32)
    weights = jnp.exp(concentration * cosine) * keep_mask[:, :, None]
    spectral = jnp.dot(
        weights.reshape(row_count * row_count, -1),
        backward,
        precision=highest,
        preferred_element_type=jnp.float32,
    ).reshape(row_count, row_count, -1)
    degree = jnp.sum(spectral[:, :, 0], axis=1)
    rounded = spectral.astype(jnp.bfloat16)
    weight_real = jnp.concatenate([rounded[:, :, :half_width], rounded[:, :, :half_width]], axis=2)
    weight_imag = jnp.concatenate([-rounded[:, :, half_width:], rounded[:, :, half_width:]], axis=2)
    filtered = jnp.einsum(
        "ijc,jrc->irc", weight_real, other_block, preferred_element_type=jnp.float32
    )
    filtered = filtered + jnp.einsum(
        "ijc,jrc->irc", weight_imag, swapped, preferred_element_type=jnp.float32
    )
    return (filtered, degree)


def body(coefficients):
    own_block = lax.all_gather(coefficients, "off", axis=1, tiled=True)
    own_inverse = inverse_norms(own_block)
    row_count, radial, angular = own_block.shape
    forward, backward = angle_tables(angular)
    ranges = lax.axis_size("off")
    per_range = min(8, lax.axis_size("blk") // ranges)
    range_index = lax.axis_index("off")
    range_base = range_index * per_range
    packet = own_block
    for bit_number in range(ranges.bit_length() - 1):
        moved_packet = shifted(packet, "blk", -(per_range << bit_number))
        chosen = range_index // (1 << bit_number) % 2 == 1
        packet = jnp.where(chosen, moved_packet, packet)
    empty_sum = jnp.zeros((row_count, radial, angular), jnp.float32)
    empty_degree = jnp.zeros((row_count,), jnp.float32)

    def advance_one(step, loop_state):
        filtered, degree, current = loop_state
        terms = tile_terms(own_block, own_inverse, current, range_base + step, forward, backward)
        current = shifted(current, "blk", -1)
        return (filtered + terms[0], degree + terms[1], current)

    last_step = per_range - 1
    filtered, degree, current = lax.fori_loop(
        0, last_step, advance_one, (empty_sum, empty_degree, packet)
    )
    terms = tile_terms(own_block, own_inverse, current, range_base + last_step, forward, backward)
    filtered = filtered + terms[0]
    degree = degree + terms[1]
    totals = (
        lax.psum_scatter(filtered, "off", scatter_dimension=0, tiled=True),
        lax.psum_scatter(degree, "off", scatter_dimension=0, tiled=True),
    )
    smoothed = totals[0] / totals[1][:, None, None]
    return (smoothed, jnp.log(totals[1]))


def solution(mesh):
    return jax.shard_map(
        body,
        mesh=mesh,
        in_specs=(P("blk", "off", None),),
        out_specs=(P(("blk", "off"), None, None), P(("blk", "off"))),
        check_vma=False,
    )
```

profile of v0, /device:TPU:1, one launch (start us, length us, event | category | flops | bytes accessed | tf_op | source)
XLA Modules:
  0.0 278.7 jit_solution(10738338174467296353)
XLA Ops:
  8.2 28.6 %all_gather.3 = bf16[16,32,128]{0,1,2:T(8,128)(2,1)S(1)} all-gather(bf16[16,8,128]{0,1,2:T(8,128)(2,1)S(1)} %copy.20), channel_id=1, replica_groups=mesh['blk'=128,'off'=4] {'off'}, dimensions={1}, use_global_device_ids=true | all-gather | bytes 163840 | tf_op jit(solution)/shard_map/all_gather | solution.py:74
  38.0 14.6 %collective-permute-start.1 = (bf16[16,32,128]{2,1,0:T(8,128)(2,1)S(1)}, bf16[16,32,128]{2,1,0:T(8,128)(2,1)S(1)}, u32[]{:S(2)}, u32[]{:S(2)}) collective-permute-start(bf16[16,32,128]{2,1,0:T(8,128)(2,1)S(1)} %copy.21), channel_id=1, source_target_pairs={{0,480},{4,484},{8,488},{12,492},{16,496},{20,500},{24,504},{28,50... | collective-permute-start | bytes 393224 | tf_op jit(solution)/shard_map/ppermute | solution.py:13
  53.4 1.9 collective-permute-done.1
  55.3 2.4 copy.22
  60.2 9.7 %collective-permute-start.2 = (bf16[16,32,128]{2,1,0:T(8,128)(2,1)S(1)}, bf16[16,32,128]{2,1,0:T(8,128)(2,1)S(1)}, u32[]{:S(2)}, u32[]{:S(2)}) collective-permute-start(bf16[16,32,128]{2,1,0:T(8,128)(2,1)S(1)} %copy.23), channel_id=1, source_target_pairs={{0,448},{4,452},{8,456},{12,460},{16,464},{20,468},{24,472},{28,47... | collective-permute-start | bytes 393224 | tf_op jit(solution)/shard_map/ppermute | solution.py:13
  71.2 1.8 collective-permute-done.2
  75.6 2.5 copy.25
  78.1 125.4 %while.18 = (s32[]{:T(128)}, f32[16,32,128]{1,0,2:T(8,128)}, f32[16]{0:T(128)}, bf16[16,32,128]{2,1,0:T(8,128)(2,1)S(1)}, bf16[16,32,128]{1,0,2:T(8,128)(2,1)S(1...) while((s32[]{:T(128)}, f32[16,32,128]{1,0,2:T(8,128)}, ...), condition=%wide.region_4.5_spmd.clone, body=%wide.region_1.4_spmd.clone.sunk | while | flops 110216208 | bytes 6230326 | solution.py:97
  78.3 16.1 %collective-permute-start = (bf16[16,32,128]{2,1,0:T(8,128)(2,1)S(1)}, bf16[16,32,128]{2,1,0:T(8,128)(2,1)S(1)}, u32[]{:S(2)}, u32[]{:S(2)}) collective-permute-start(bf16[16,32,128]{2,1,0:T(8,128)(2,1)S(1)} %copy.56), channel_id=1, source_target_pairs={{0,508},{4,0},{8,4},{12,8},{16,12},{20,16},{24,20},{28,24},{32,28}... | collective-permute-start | bytes 393224 | tf_op jit(solution)/shard_map/while/body/eval_jaxpr/ppermute | solution.py:13
  102.4 9.1 %collective-permute-start = (bf16[16,32,128]{2,1,0:T(8,128)(2,1)S(1)}, bf16[16,32,128]{2,1,0:T(8,128)(2,1)S(1)}, u32[]{:S(2)}, u32[]{:S(2)}) collective-permute-start(bf16[16,32,128]{2,1,0:T(8,128)(2,1)S(1)} %copy.56), channel_id=1, source_target_pairs={{0,508},{4,0},{8,4},{12,8},{16,12},{20,16},{24,20},{28,24},{32,28}... | collective-permute-start | bytes 393224 | tf_op jit(solution)/shard_map/while/body/eval_jaxpr/ppermute | solution.py:13
  117.5 2.7 fusion.95
  120.8 7.3 %collective-permute-start = (bf16[16,32,128]{2,1,0:T(8,128)(2,1)S(1)}, bf16[16,32,128]{2,1,0:T(8,128)(2,1)S(1)}, u32[]{:S(2)}, u32[]{:S(2)}) collective-permute-start(bf16[16,32,128]{2,1,0:T(8,128)(2,1)S(1)} %copy.56), channel_id=1, source_target_pairs={{0,508},{4,0},{8,4},{12,8},{16,12},{20,16},{24,20},{28,24},{32,28}... | collective-permute-start | bytes 393224 | tf_op jit(solution)/shard_map/while/body/eval_jaxpr/ppermute | solution.py:13
  134.1 2.7 fusion.95
  137.3 7.3 %collective-permute-start = (bf16[16,32,128]{2,1,0:T(8,128)(2,1)S(1)}, bf16[16,32,128]{2,1,0:T(8,128)(2,1)S(1)}, u32[]{:S(2)}, u32[]{:S(2)}) collective-permute-start(bf16[16,32,128]{2,1,0:T(8,128)(2,1)S(1)} %copy.56), channel_id=1, source_target_pairs={{0,508},{4,0},{8,4},{12,8},{16,12},{20,16},{24,20},{28,24},{32,28}... | collective-permute-start | bytes 393224 | tf_op jit(solution)/shard_map/while/body/eval_jaxpr/ppermute | solution.py:13
  150.6 2.7 fusion.95
  153.9 7.3 %collective-permute-start = (bf16[16,32,128]{2,1,0:T(8,128)(2,1)S(1)}, bf16[16,32,128]{2,1,0:T(8,128)(2,1)S(1)}, u32[]{:S(2)}, u32[]{:S(2)}) collective-permute-start(bf16[16,32,128]{2,1,0:T(8,128)(2,1)S(1)} %copy.56), channel_id=1, source_target_pairs={{0,508},{4,0},{8,4},{12,8},{16,12},{20,16},{24,20},{28,24},{32,28}... | collective-permute-start | bytes 393224 | tf_op jit(solution)/shard_map/while/body/eval_jaxpr/ppermute | solution.py:13
  167.2 2.7 fusion.95
  170.5 7.3 %collective-permute-start = (bf16[16,32,128]{2,1,0:T(8,128)(2,1)S(1)}, bf16[16,32,128]{2,1,0:T(8,128)(2,1)S(1)}, u32[]{:S(2)}, u32[]{:S(2)}) collective-permute-start(bf16[16,32,128]{2,1,0:T(8,128)(2,1)S(1)} %copy.56), channel_id=1, source_target_pairs={{0,508},{4,0},{8,4},{12,8},{16,12},{20,16},{24,20},{28,24},{32,28}... | collective-permute-start | bytes 393224 | tf_op jit(solution)/shard_map/while/body/eval_jaxpr/ppermute | solution.py:13
  183.7 2.7 fusion.95
  187.0 7.3 %collective-permute-start = (bf16[16,32,128]{2,1,0:T(8,128)(2,1)S(1)}, bf16[16,32,128]{2,1,0:T(8,128)(2,1)S(1)}, u32[]{:S(2)}, u32[]{:S(2)}) collective-permute-start(bf16[16,32,128]{2,1,0:T(8,128)(2,1)S(1)} %copy.56), channel_id=1, source_target_pairs={{0,508},{4,0},{8,4},{12,8},{16,12},{20,16},{24,20},{28,24},{32,28}... | collective-permute-start | bytes 393224 | tf_op jit(solution)/shard_map/while/body/eval_jaxpr/ppermute | solution.py:13
  200.3 2.7 fusion.95
  210.1 1.6 fusion.17
  215.0 21.4 %all-reduce = f32[16]{0:T(128)S(1)} all-reduce(f32[16]{0:T(128)S(1)} %add.125), channel_id=3, replica_groups=mesh['blk'=128,'off'=4] {'off'}, use_global_device_ids=true, to_apply=%region_8.9.clone | all-reduce | flops 16 | bytes 128
  237.0 33.3 %reduce-scatter.2.cloned.1.call-done = f32[4,32,128]{2,1,0:T(8,128)} async-done(((f32[16,32,128]{2,1,0:T(8,128)}), f32[4,32,128]{2,1,0:T(8,128)}) %reduce-scatter.2.cloned.1.call-update) | async-done | bytes 65552 | tf_op jit(solution)/shard_map/reduce_scatter | solution.py:104
  (256 shorter events, 66.7 us)
Async XLA Ops:
  7.2 263.1 %reduce-scatter.2.cloned.1.call-start = ((), (), s32[]{:S(2)}) async-start(), calls=%async_computation.1 | async-start | bytes 327680 | tf_op jit(solution)/shard_map/reduce_scatter | solution.py:104
  36.8 33.2 %copy-start = (bf16[16,32,128]{0,1,2:T(8,128)(2,1)}, bf16[16,32,128]{0,1,2:T(8,128)(2,1)S(1)}, u32[]{:S(2)}) copy-start(bf16[16,32,128]{0,1,2:T(8,128)(2,1)S(1)} %all_gather.3) | copy-start | bytes 393220
  38.0 17.3 %collective-permute-start.1 = (bf16[16,32,128]{2,1,0:T(8,128)(2,1)S(1)}, bf16[16,32,128]{2,1,0:T(8,128)(2,1)S(1)}, u32[]{:S(2)}, u32[]{:S(2)}) collective-permute-start(bf16[16,32,128]{2,1,0:T(8,128)(2,1)S(1)} %copy.21), channel_id=1, source_target_pairs={{0,480},{4,484},{8,488},{12,492},{16,496},{20,500},{24,504},{28,50... | collective-permute-start | bytes 393224 | tf_op jit(solution)/shard_map/ppermute | solution.py:13
  53.3 16.6 %copy-start.3 = (f32[64,128]{1,0:T(8,128)}, f32[64,128]{1,0:T(8,128)S(1)}, u32[]{:S(2)}) copy-start(f32[64,128]{1,0:T(8,128)S(1)} %get-tuple-element.249) | copy-start | bytes 98308
  53.3 16.6 %copy-start.5 = (f32[64,128]{1,0:T(8,128)}, f32[64,128]{1,0:T(8,128)S(1)}, u32[]{:S(2)}) copy-start(f32[64,128]{1,0:T(8,128)S(1)} %get-tuple-element.250) | copy-start | bytes 98308
  60.2 12.8 %collective-permute-start.2 = (bf16[16,32,128]{2,1,0:T(8,128)(2,1)S(1)}, bf16[16,32,128]{2,1,0:T(8,128)(2,1)S(1)}, u32[]{:S(2)}, u32[]{:S(2)}) collective-permute-start(bf16[16,32,128]{2,1,0:T(8,128)(2,1)S(1)} %copy.23), channel_id=1, source_target_pairs={{0,448},{4,452},{8,456},{12,460},{16,464},{20,468},{24,472},{28,47... | collective-permute-start | bytes 393224 | tf_op jit(solution)/shard_map/ppermute | solution.py:13
  78.3 23.6 %collective-permute-start = (bf16[16,32,128]{2,1,0:T(8,128)(2,1)S(1)}, bf16[16,32,128]{2,1,0:T(8,128)(2,1)S(1)}, u32[]{:S(2)}, u32[]{:S(2)}) collective-permute-start(bf16[16,32,128]{2,1,0:T(8,128)(2,1)S(1)} %copy.56), channel_id=1, source_target_pairs={{0,508},{4,0},{8,4},{12,8},{16,12},{20,16},{24,20},{28,24},{32,28}... | collective-permute-start | bytes 393224 | tf_op jit(solution)/shard_map/while/body/eval_jaxpr/ppermute | solution.py:13
  100.4 1.5 copy-start.7
  102.4 17.8 %collective-permute-start = (bf16[16,32,128]{2,1,0:T(8,128)(2,1)S(1)}, bf16[16,32,128]{2,1,0:T(8,128)(2,1)S(1)}, u32[]{:S(2)}, u32[]{:S(2)}) collective-permute-start(bf16[16,32,128]{2,1,0:T(8,128)(2,1)S(1)} %copy.56), channel_id=1, source_target_pairs={{0,508},{4,0},{8,4},{12,8},{16,12},{20,16},{24,20},{28,24},{32,28}... | collective-permute-start | bytes 393224 | tf_op jit(solution)/shard_map/while/body/eval_jaxpr/ppermute | solution.py:13
  117.5 2.7 copy-start.7
  120.8 16.0 %collective-permute-start = (bf16[16,32,128]{2,1,0:T(8,128)(2,1)S(1)}, bf16[16,32,128]{2,1,0:T(8,128)(2,1)S(1)}, u32[]{:S(2)}, u32[]{:S(2)}) collective-permute-start(bf16[16,32,128]{2,1,0:T(8,128)(2,1)S(1)} %copy.56), channel_id=1, source_target_pairs={{0,508},{4,0},{8,4},{12,8},{16,12},{20,16},{24,20},{28,24},{32,28}... | collective-permute-start | bytes 393224 | tf_op jit(solution)/shard_map/while/body/eval_jaxpr/ppermute | solution.py:13
  134.1 2.7 copy-start.7
  137.3 16.0 %collective-permute-start = (bf16[16,32,128]{2,1,0:T(8,128)(2,1)S(1)}, bf16[16,32,128]{2,1,0:T(8,128)(2,1)S(1)}, u32[]{:S(2)}, u32[]{:S(2)}) collective-permute-start(bf16[16,32,128]{2,1,0:T(8,128)(2,1)S(1)} %copy.56), channel_id=1, source_target_pairs={{0,508},{4,0},{8,4},{12,8},{16,12},{20,16},{24,20},{28,24},{32,28}... | collective-permute-start | bytes 393224 | tf_op jit(solution)/shard_map/while/body/eval_jaxpr/ppermute | solution.py:13
  150.6 2.7 copy-start.7
  153.9 16.0 %collective-permute-start = (bf16[16,32,128]{2,1,0:T(8,128)(2,1)S(1)}, bf16[16,32,128]{2,1,0:T(8,128)(2,1)S(1)}, u32[]{:S(2)}, u32[]{:S(2)}) collective-permute-start(bf16[16,32,128]{2,1,0:T(8,128)(2,1)S(1)} %copy.56), channel_id=1, source_target_pairs={{0,508},{4,0},{8,4},{12,8},{16,12},{20,16},{24,20},{28,24},{32,28}... | collective-permute-start | bytes 393224 | tf_op jit(solution)/shard_map/while/body/eval_jaxpr/ppermute | solution.py:13
  167.2 2.7 copy-start.7
  170.5 16.0 %collective-permute-start = (bf16[16,32,128]{2,1,0:T(8,128)(2,1)S(1)}, bf16[16,32,128]{2,1,0:T(8,128)(2,1)S(1)}, u32[]{:S(2)}, u32[]{:S(2)}) collective-permute-start(bf16[16,32,128]{2,1,0:T(8,128)(2,1)S(1)} %copy.56), channel_id=1, source_target_pairs={{0,508},{4,0},{8,4},{12,8},{16,12},{20,16},{24,20},{28,24},{32,28}... | collective-permute-start | bytes 393224 | tf_op jit(solution)/shard_map/while/body/eval_jaxpr/ppermute | solution.py:13
  183.7 2.7 copy-start.7
  187.0 16.0 %collective-permute-start = (bf16[16,32,128]{2,1,0:T(8,128)(2,1)S(1)}, bf16[16,32,128]{2,1,0:T(8,128)(2,1)S(1)}, u32[]{:S(2)}, u32[]{:S(2)}) collective-permute-start(bf16[16,32,128]{2,1,0:T(8,128)(2,1)S(1)} %copy.56), channel_id=1, source_target_pairs={{0,508},{4,0},{8,4},{12,8},{16,12},{20,16},{24,20},{28,24},{32,28}... | collective-permute-start | bytes 393224 | tf_op jit(solution)/shard_map/while/body/eval_jaxpr/ppermute | solution.py:13
  200.3 2.7 copy-start.7
  203.7 1.2 copy-start.1
  206.2 0.8 copy-start.6
  208.2 1.9 copy-start.2
  211.7 3.3 %copy-start.9 = (f32[16]{0:T(128)S(1)}, f32[16]{0:T(128)}, u32[]{:S(2)}) copy-start(f32[16]{0:T(128)} %get-tuple-element.160) | copy-start | bytes 196
  (8 other events, 4.8 us)
Sparse Core Ops, SparseCore 0:
  213.0 57.2 reduce-scatter.1
where the time goes:
time: 280 us; the launch traced here: 279 us
  starting transfers between devices  86.1 us (31%)
  blocking collectives  50 us (18%)
  matrix products  40.1 us (14%)
  local copies, waits for them, and re-layouts  37.3 us (13%)
  waiting for transfers between devices  37.1 us (13%)
  between operations  15 us (5%)
  other arithmetic  11.9 us (4%)
    ppermute x9, starting transfers between devices, shifted(): lax.ppermute(array, axis, [(i, (i + by) % count) for i in range(count)])  86.1 us
    reduce_scatter x1, waiting for transfers between devices, body(): lax.psum_scatter(filtered, 'off', scatter_dimension=0, tiled=True)  33.3 us
    all_gather x1, blocking collectives, body(): own_block = lax.all_gather(coefficients, 'off', axis=1, tiled=True)  28.6 us
    unnamed x1, blocking collectives  21.4 us
    dot_general x8, matrix products, tile_terms(): jnp.einsum('ijc,jrc->irc', weight_imag, swapped, preferred_element_type=j...  19.2 us
    dot_general x8, matrix products, tile_terms(): jnp.dot(weights.reshape(row_count * row_count, -1), backward, precision=h...  7.98 us
    while x42, local copies, waits for them, and re-layouts  7.01 us
    unnamed x21, local copies, waits for them, and re-layouts  6.46 us
  transfers between devices with their start and end apart: 10, of which 3 were waited for; matrix products, arithmetic and copies ran while one was open for 22% of the time, Pallas kernels for 0%

commit v1 on v0

--- a/solution.py
+++ b/solution.py
@@ -6,6 +6,11 @@
 
 epsilon = 1e-06
 concentration = 40.0
+
+
+def gathered_along(x, axis, d):
+    blocks = lax.all_gather(x, axis)
+    return jnp.concatenate(blocks, axis=d)
 
 
 def shifted(array, axis, by):
@@ -71,7 +76,7 @@
 
 
 def body(coefficients):
-    own_block = lax.all_gather(coefficients, "off", axis=1, tiled=True)
+    own_block = gathered_along(coefficients, "off", 1)
     own_inverse = inverse_norms(own_block)
     row_count, radial, angular = own_block.shape
     forward, backward = angle_tables(angular)

time: 280 us -> 250 us (0.89)
  matrix products: 40.1 us -> 32 us
  blocking collectives: 50 us -> 44 us
  local copies, waits for them, and re-layouts: 37.3 us -> 32.2 us
  starting transfers between devices: 86.1 us -> 81.9 us
  waiting for transfers between devices: 37.1 us -> 33.7 us
    all_gather x1, blocking collectives: 28.6 us -> 21 us  [gathered_along(): blocks = lax.all_gather(x, axis)]
    dot_general x8, matrix products: 7.98 us -> 2.11 us  [tile_terms(): jnp.dot(weights.reshape(row_count * row_count, -1), backward, precision=h...]
    ppermute x9, starting transfers between devices: 86.1 us -> 81.9 us  [shifted(): lax.ppermute(array, axis, [(i, (i + by) % count) for i in range(count)])]
    reduce_scatter x1, waiting for transfers between devices: 33.3 us -> 29.3 us  [body(): lax.psum_scatter(filtered, 'off', scatter_dimension=0, tiled=True)]
    ppermute x2 -> x0, local copies, waits for them, and re-layouts: 3.87 us -> none  [shifted(): lax.ppermute(array, axis, [(i, (i + by) % count) for i in range(count)])]
    while x42 -> x70, local copies, waits for them, and re-layouts: 7.01 us -> 10.8 us
    unnamed x21 -> x15, local copies, waits for them, and re-layouts: 6.46 us -> 3.68 us
where the time goes in v1:
time: 250 us; the launch traced here: 249 us
  starting transfers between devices  81.9 us (33%)
  blocking collectives  44 us (18%)
  waiting for transfers between devices  33.7 us (13%)
  local copies, waits for them, and re-layouts  32.2 us (13%)
  matrix products  32 us (13%)
  between operations  15 us (6%)
  other arithmetic  9.28 us (4%)
    ppermute x9, starting transfers between devices, shifted(): lax.ppermute(array, axis, [(i, (i + by) % count) for i in range(count)])  81.9 us
    reduce_scatter x1, waiting for transfers between devices, body(): lax.psum_scatter(filtered, 'off', scatter_dimension=0, tiled=True)  29.3 us
    unnamed x1, blocking collectives  23 us
    all_gather x1, blocking collectives, gathered_along(): blocks = lax.all_gather(x, axis)  21 us
    dot_general x8, matrix products, tile_terms(): jnp.einsum('ijc,jrc->irc', weight_imag, swapped, preferred_element_type=j...  17.8 us
    while x70, local copies, waits for them, and re-layouts  10.8 us
  transfers between devices with their start and end apart: 10, of which 3 were waited for; matrix products, arithmetic and copies ran while one was open for 22% of the time, Pallas kernels for 0%

profile of v1, /device:TPU:1, one launch (start us, length us, event | category | flops | bytes accessed | tf_op | source)
XLA Modules:
  0.0 249.0 jit_solution(8697174802594981260)
XLA Ops:
  7.2 21.0 %all-gather = bf16[64,8,128]{2,1,0:T(8,128)(2,1)S(1)} all-gather(bf16[16,8,128]{2,1,0:T(8,128)(2,1)} %param.3), channel_id=2, replica_groups=mesh['blk'=128,'off'=4] {'off'}, dimensions={0}, use_global_device_ids=true | all-gather | bytes 163840 | tf_op jit(solution)/shard_map/all_gather | solution.py:12
  28.3 10.2 %collective-permute-start.1 = (bf16[16,32,128]{2,1,0:T(8,128)(2,1)S(1)}, bf16[16,32,128]{2,1,0:T(8,128)(2,1)S(1)}, u32[]{:S(2)}, u32[]{:S(2)}) collective-permute-start(bf16[16,32,128]{2,1,0:T(8,128)(2,1)S(1)} %copy_bitcast_fusion), channel_id=1, source_target_pairs={{0,480},{4,484},{8,488},{12,492},{16,496},{20,500},{24,504},{28,50... | collective-permute-start | bytes 393224 | tf_op jit(solution)/shard_map/ppermute | solution.py:18
  38.8 2.3 collective-permute-done.1
  41.1 3.0 %collective-permute-start.2 = (bf16[16,32,128]{2,1,0:T(8,128)(2,1)S(1)}, bf16[16,32,128]{2,1,0:T(8,128)(2,1)S(1)}, u32[]{:S(2)}, u32[]{:S(2)}) collective-permute-start(bf16[16,32,128]{2,1,0:T(8,128)(2,1)S(1)} %broadcast_select_fusion.1), channel_id=1, source_target_pairs={{0,448},{4,452},{8,456},{12,460},{16,464},{20,468},{24,472},{28,47... | collective-permute-start | bytes 393224 | tf_op jit(solution)/shard_map/ppermute | solution.py:18
  44.8 2.1 collective-permute-done.2
  46.9 130.2 %while.18 = (s32[]{:T(128)}, f32[16,32,128]{1,0,2:T(8,128)}, f32[16]{0:T(128)}, bf16[16,32,128]{2,1,0:T(8,128)(2,1)S(1)}, bf16[16,32,128]{1,0,2:T(8,128)(2,1)S(1...) while((s32[]{:T(128)}, f32[16,32,128]{1,0,2:T(8,128)}, ...), condition=%wide.region_4.5_spmd.clone, body=%wide.region_1.4_spmd.clone.sunk | while | flops 110216208 | bytes 6754670 | solution.py:102
  46.9 21.7 %collective-permute-start = (bf16[16,32,128]{2,1,0:T(8,128)(2,1)S(1)}, bf16[16,32,128]{2,1,0:T(8,128)(2,1)S(1)}, u32[]{:S(2)}, u32[]{:S(2)}) collective-permute-start(bf16[16,32,128]{2,1,0:T(8,128)(2,1)S(1)} %copy.77), channel_id=1, source_target_pairs={{0,508},{4,0},{8,4},{12,8},{16,12},{20,16},{24,20},{28,24},{32,28}... | collective-permute-start | bytes 393224 | tf_op jit(solution)/shard_map/while/body/eval_jaxpr/ppermute | solution.py:18
  73.8 1.4 fusion.96
  76.3 8.9 %collective-permute-start = (bf16[16,32,128]{2,1,0:T(8,128)(2,1)S(1)}, bf16[16,32,128]{2,1,0:T(8,128)(2,1)S(1)}, u32[]{:S(2)}, u32[]{:S(2)}) collective-permute-start(bf16[16,32,128]{2,1,0:T(8,128)(2,1)S(1)} %copy.77), channel_id=1, source_target_pairs={{0,508},{4,0},{8,4},{12,8},{16,12},{20,16},{24,20},{28,24},{32,28}... | collective-permute-start | bytes 393224 | tf_op jit(solution)/shard_map/while/body/eval_jaxpr/ppermute | solution.py:18
  90.4 2.7 %fusion.96 = f32[16,32,128]{1,0,2:T(8,128)} fusion(f32[16,32,128]{1,0,2:T(8,128)S(1)} %convolution_bitcast_fusion.11, bf16[16,16,128]{1,0,2:T(8,128)(2,1)S(1)} %copy.69, bf16[16,32,128]{1,0,2:T(8,128)(2,1)S(1)} %copy.64, f32[16,32,128]{1,0,2:T(8,128)} %get-tuple-element.358, pred[]{:T(512)S(6)} %compare.9), kind=kOutput, calls=%fused_computation.2.clone.1 | convolution fusion | flops 2293760 | bytes 983041 | tf_op jit(solution)/shard_map/while/body/eval_jaxpr/ijc,jrc->irc/dot_general | solution.py:72
  94.2 7.6 %collective-permute-start = (bf16[16,32,128]{2,1,0:T(8,128)(2,1)S(1)}, bf16[16,32,128]{2,1,0:T(8,128)(2,1)S(1)}, u32[]{:S(2)}, u32[]{:S(2)}) collective-permute-start(bf16[16,32,128]{2,1,0:T(8,128)(2,1)S(1)} %copy.77), channel_id=1, source_target_pairs={{0,508},{4,0},{8,4},{12,8},{16,12},{20,16},{24,20},{28,24},{32,28}... | collective-permute-start | bytes 393224 | tf_op jit(solution)/shard_map/while/body/eval_jaxpr/ppermute | solution.py:18
  106.9 2.7 %fusion.96 = f32[16,32,128]{1,0,2:T(8,128)} fusion(f32[16,32,128]{1,0,2:T(8,128)S(1)} %convolution_bitcast_fusion.11, bf16[16,16,128]{1,0,2:T(8,128)(2,1)S(1)} %copy.69, bf16[16,32,128]{1,0,2:T(8,128)(2,1)S(1)} %copy.64, f32[16,32,128]{1,0,2:T(8,128)} %get-tuple-element.358, pred[]{:T(512)S(6)} %compare.9), kind=kOutput, calls=%fused_computation.2.clone.1 | convolution fusion | flops 2293760 | bytes 983041 | tf_op jit(solution)/shard_map/while/body/eval_jaxpr/ijc,jrc->irc/dot_general | solution.py:72
  110.7 7.6 %collective-permute-start = (bf16[16,32,128]{2,1,0:T(8,128)(2,1)S(1)}, bf16[16,32,128]{2,1,0:T(8,128)(2,1)S(1)}, u32[]{:S(2)}, u32[]{:S(2)}) collective-permute-start(bf16[16,32,128]{2,1,0:T(8,128)(2,1)S(1)} %copy.77), channel_id=1, source_target_pairs={{0,508},{4,0},{8,4},{12,8},{16,12},{20,16},{24,20},{28,24},{32,28}... | collective-permute-start | bytes 393224 | tf_op jit(solution)/shard_map/while/body/eval_jaxpr/ppermute | solution.py:18
  123.5 2.7 %fusion.96 = f32[16,32,128]{1,0,2:T(8,128)} fusion(f32[16,32,128]{1,0,2:T(8,128)S(1)} %convolution_bitcast_fusion.11, bf16[16,16,128]{1,0,2:T(8,128)(2,1)S(1)} %copy.69, bf16[16,32,128]{1,0,2:T(8,128)(2,1)S(1)} %copy.64, f32[16,32,128]{1,0,2:T(8,128)} %get-tuple-element.358, pred[]{:T(512)S(6)} %compare.9), kind=kOutput, calls=%fused_computation.2.clone.1 | convolution fusion | flops 2293760 | bytes 983041 | tf_op jit(solution)/shard_map/while/body/eval_jaxpr/ijc,jrc->irc/dot_general | solution.py:72
  127.3 7.6 %collective-permute-start = (bf16[16,32,128]{2,1,0:T(8,128)(2,1)S(1)}, bf16[16,32,128]{2,1,0:T(8,128)(2,1)S(1)}, u32[]{:S(2)}, u32[]{:S(2)}) collective-permute-start(bf16[16,32,128]{2,1,0:T(8,128)(2,1)S(1)} %copy.77), channel_id=1, source_target_pairs={{0,508},{4,0},{8,4},{12,8},{16,12},{20,16},{24,20},{28,24},{32,28}... | collective-permute-start | bytes 393224 | tf_op jit(solution)/shard_map/while/body/eval_jaxpr/ppermute | solution.py:18
  140.0 2.7 %fusion.96 = f32[16,32,128]{1,0,2:T(8,128)} fusion(f32[16,32,128]{1,0,2:T(8,128)S(1)} %convolution_bitcast_fusion.11, bf16[16,16,128]{1,0,2:T(8,128)(2,1)S(1)} %copy.69, bf16[16,32,128]{1,0,2:T(8,128)(2,1)S(1)} %copy.64, f32[16,32,128]{1,0,2:T(8,128)} %get-tuple-element.358, pred[]{:T(512)S(6)} %compare.9), kind=kOutput, calls=%fused_computation.2.clone.1 | convolution fusion | flops 2293760 | bytes 983041 | tf_op jit(solution)/shard_map/while/body/eval_jaxpr/ijc,jrc->irc/dot_general | solution.py:72
  143.8 7.6 %collective-permute-start = (bf16[16,32,128]{2,1,0:T(8,128)(2,1)S(1)}, bf16[16,32,128]{2,1,0:T(8,128)(2,1)S(1)}, u32[]{:S(2)}, u32[]{:S(2)}) collective-permute-start(bf16[16,32,128]{2,1,0:T(8,128)(2,1)S(1)} %copy.77), channel_id=1, source_target_pairs={{0,508},{4,0},{8,4},{12,8},{16,12},{20,16},{24,20},{28,24},{32,28}... | collective-permute-start | bytes 393224 | tf_op jit(solution)/shard_map/while/body/eval_jaxpr/ppermute | solution.py:18
  156.6 2.7 %fusion.96 = f32[16,32,128]{1,0,2:T(8,128)} fusion(f32[16,32,128]{1,0,2:T(8,128)S(1)} %convolution_bitcast_fusion.11, bf16[16,16,128]{1,0,2:T(8,128)(2,1)S(1)} %copy.69, bf16[16,32,128]{1,0,2:T(8,128)(2,1)S(1)} %copy.64, f32[16,32,128]{1,0,2:T(8,128)} %get-tuple-element.358, pred[]{:T(512)S(6)} %compare.9), kind=kOutput, calls=%fused_computation.2.clone.1 | convolution fusion | flops 2293760 | bytes 983041 | tf_op jit(solution)/shard_map/while/body/eval_jaxpr/ijc,jrc->irc/dot_general | solution.py:72
  160.4 7.7 %collective-permute-start = (bf16[16,32,128]{2,1,0:T(8,128)(2,1)S(1)}, bf16[16,32,128]{2,1,0:T(8,128)(2,1)S(1)}, u32[]{:S(2)}, u32[]{:S(2)}) collective-permute-start(bf16[16,32,128]{2,1,0:T(8,128)(2,1)S(1)} %copy.77), channel_id=1, source_target_pairs={{0,508},{4,0},{8,4},{12,8},{16,12},{20,16},{24,20},{28,24},{32,28}... | collective-permute-start | bytes 393224 | tf_op jit(solution)/shard_map/while/body/eval_jaxpr/ppermute | solution.py:18
  173.3 2.7 %fusion.96 = f32[16,32,128]{1,0,2:T(8,128)} fusion(f32[16,32,128]{1,0,2:T(8,128)S(1)} %convolution_bitcast_fusion.11, bf16[16,16,128]{1,0,2:T(8,128)(2,1)S(1)} %copy.69, bf16[16,32,128]{1,0,2:T(8,128)(2,1)S(1)} %copy.64, f32[16,32,128]{1,0,2:T(8,128)} %get-tuple-element.358, pred[]{:T(512)S(6)} %compare.9), kind=kOutput, calls=%fused_computation.2.clone.1 | convolution fusion | flops 2293760 | bytes 983041 | tf_op jit(solution)/shard_map/while/body/eval_jaxpr/ijc,jrc->irc/dot_general | solution.py:72
  185.1 1.3 dynamic-slice
  187.8 23.0 %all-reduce = f32[16]{0:T(128)S(1)} all-reduce(f32[16]{0:T(128)S(1)} %add.125), channel_id=4, replica_groups=mesh['blk'=128,'off'=4] {'off'}, use_global_device_ids=true, to_apply=%region_8.9.clone | all-reduce | flops 16 | bytes 128
  211.4 29.3 %reduce-scatter.2.cloned.1.call-done = f32[4,32,128]{2,1,0:T(8,128)} async-done(((f32[16,32,128]{2,1,0:T(8,128)}), f32[4,32,128]{2,1,0:T(8,128)}) %reduce-scatter.2.cloned.1.call-update) | async-done | bytes 65552 | tf_op jit(solution)/shard_map/reduce_scatter | solution.py:109
  240.6 1.5 broadcast_divide_fusion
  (276 shorter events, 53.2 us)
Async XLA Ops:
  7.2 233.5 %reduce-scatter.2.cloned.1.call-start = ((), (), s32[]{:S(2)}) async-start(), calls=%async_computation.1 | async-start | bytes 327680 | tf_op jit(solution)/shard_map/reduce_scatter | solution.py:109
  28.3 12.8 %collective-permute-start.1 = (bf16[16,32,128]{2,1,0:T(8,128)(2,1)S(1)}, bf16[16,32,128]{2,1,0:T(8,128)(2,1)S(1)}, u32[]{:S(2)}, u32[]{:S(2)}) collective-permute-start(bf16[16,32,128]{2,1,0:T(8,128)(2,1)S(1)} %copy_bitcast_fusion), channel_id=1, source_target_pairs={{0,480},{4,484},{8,488},{12,492},{16,496},{20,500},{24,504},{28,50... | collective-permute-start | bytes 393224 | tf_op jit(solution)/shard_map/ppermute | solution.py:18
  38.8 5.3 %copy-start.3 = (f32[64,128]{1,0:T(8,128)}, f32[64,128]{1,0:T(8,128)S(1)}, u32[]{:S(2)}) copy-start(f32[64,128]{1,0:T(8,128)S(1)} %get-tuple-element.271) | copy-start | bytes 98308
  38.8 5.3 %copy-start.5 = (f32[64,128]{1,0:T(8,128)}, f32[64,128]{1,0:T(8,128)S(1)}, u32[]{:S(2)}) copy-start(f32[64,128]{1,0:T(8,128)S(1)} %get-tuple-element.272) | copy-start | bytes 98308
  41.1 5.7 %collective-permute-start.2 = (bf16[16,32,128]{2,1,0:T(8,128)(2,1)S(1)}, bf16[16,32,128]{2,1,0:T(8,128)(2,1)S(1)}, u32[]{:S(2)}, u32[]{:S(2)}) collective-permute-start(bf16[16,32,128]{2,1,0:T(8,128)(2,1)S(1)} %broadcast_select_fusion.1), channel_id=1, source_target_pairs={{0,448},{4,452},{8,456},{12,460},{16,464},{20,468},{24,472},{28,47... | collective-permute-start | bytes 393224 | tf_op jit(solution)/shard_map/ppermute | solution.py:18
  46.9 24.9 %copy-start.1 = (f32[128,128]{1,0:T(8,128)}, f32[128,128]{1,0:T(8,128)S(1)}, u32[]{:S(2)}) copy-start(f32[128,128]{1,0:T(8,128)S(1)} %get-tuple-element.376) | copy-start | bytes 196612 | tf_op jit(solution)/shard_map/while
  46.9 28.9 %collective-permute-start = (bf16[16,32,128]{2,1,0:T(8,128)(2,1)S(1)}, bf16[16,32,128]{2,1,0:T(8,128)(2,1)S(1)}, u32[]{:S(2)}, u32[]{:S(2)}) collective-permute-start(bf16[16,32,128]{2,1,0:T(8,128)(2,1)S(1)} %copy.77), channel_id=1, source_target_pairs={{0,508},{4,0},{8,4},{12,8},{16,12},{20,16},{24,20},{28,24},{32,28}... | collective-permute-start | bytes 393224 | tf_op jit(solution)/shard_map/while/body/eval_jaxpr/ppermute | solution.py:18
  76.3 12.1 %copy-start.1 = (f32[128,128]{1,0:T(8,128)}, f32[128,128]{1,0:T(8,128)S(1)}, u32[]{:S(2)}) copy-start(f32[128,128]{1,0:T(8,128)S(1)} %get-tuple-element.376) | copy-start | bytes 196612 | tf_op jit(solution)/shard_map/while
  76.3 17.3 %collective-permute-start = (bf16[16,32,128]{2,1,0:T(8,128)(2,1)S(1)}, bf16[16,32,128]{2,1,0:T(8,128)(2,1)S(1)}, u32[]{:S(2)}, u32[]{:S(2)}) collective-permute-start(bf16[16,32,128]{2,1,0:T(8,128)(2,1)S(1)} %copy.77), channel_id=1, source_target_pairs={{0,508},{4,0},{8,4},{12,8},{16,12},{20,16},{24,20},{28,24},{32,28}... | collective-permute-start | bytes 393224 | tf_op jit(solution)/shard_map/while/body/eval_jaxpr/ppermute | solution.py:18
  90.4 3.8 %copy-start.2 = (f32[128,128]{1,0:T(8,128)S(1)}, f32[128,128]{1,0:T(8,128)}, u32[]{:S(2)}) copy-start(f32[128,128]{1,0:T(8,128)} %copy-done.1) | copy-start | bytes 196612 | tf_op jit(solution)/shard_map/while
  94.1 10.8 %copy-start.1 = (f32[128,128]{1,0:T(8,128)}, f32[128,128]{1,0:T(8,128)S(1)}, u32[]{:S(2)}) copy-start(f32[128,128]{1,0:T(8,128)S(1)} %get-tuple-element.376) | copy-start | bytes 196612 | tf_op jit(solution)/shard_map/while
  94.2 16.0 %collective-permute-start = (bf16[16,32,128]{2,1,0:T(8,128)(2,1)S(1)}, bf16[16,32,128]{2,1,0:T(8,128)(2,1)S(1)}, u32[]{:S(2)}, u32[]{:S(2)}) collective-permute-start(bf16[16,32,128]{2,1,0:T(8,128)(2,1)S(1)} %copy.77), channel_id=1, source_target_pairs={{0,508},{4,0},{8,4},{12,8},{16,12},{20,16},{24,20},{28,24},{32,28}... | collective-permute-start | bytes 393224 | tf_op jit(solution)/shard_map/while/body/eval_jaxpr/ppermute | solution.py:18
  106.9 3.8 %copy-start.2 = (f32[128,128]{1,0:T(8,128)S(1)}, f32[128,128]{1,0:T(8,128)}, u32[]{:S(2)}) copy-start(f32[128,128]{1,0:T(8,128)} %copy-done.1) | copy-start | bytes 196612 | tf_op jit(solution)/shard_map/while
  110.7 10.8 %copy-start.1 = (f32[128,128]{1,0:T(8,128)}, f32[128,128]{1,0:T(8,128)S(1)}, u32[]{:S(2)}) copy-start(f32[128,128]{1,0:T(8,128)S(1)} %get-tuple-element.376) | copy-start | bytes 196612 | tf_op jit(solution)/shard_map/while
  110.7 16.0 %collective-permute-start = (bf16[16,32,128]{2,1,0:T(8,128)(2,1)S(1)}, bf16[16,32,128]{2,1,0:T(8,128)(2,1)S(1)}, u32[]{:S(2)}, u32[]{:S(2)}) collective-permute-start(bf16[16,32,128]{2,1,0:T(8,128)(2,1)S(1)} %copy.77), channel_id=1, source_target_pairs={{0,508},{4,0},{8,4},{12,8},{16,12},{20,16},{24,20},{28,24},{32,28}... | collective-permute-start | bytes 393224 | tf_op jit(solution)/shard_map/while/body/eval_jaxpr/ppermute | solution.py:18
  123.5 3.8 %copy-start.2 = (f32[128,128]{1,0:T(8,128)S(1)}, f32[128,128]{1,0:T(8,128)}, u32[]{:S(2)}) copy-start(f32[128,128]{1,0:T(8,128)} %copy-done.1) | copy-start | bytes 196612 | tf_op jit(solution)/shard_map/while
  127.3 10.8 %copy-start.1 = (f32[128,128]{1,0:T(8,128)}, f32[128,128]{1,0:T(8,128)S(1)}, u32[]{:S(2)}) copy-start(f32[128,128]{1,0:T(8,128)S(1)} %get-tuple-element.376) | copy-start | bytes 196612 | tf_op jit(solution)/shard_map/while
  127.3 16.0 %collective-permute-start = (bf16[16,32,128]{2,1,0:T(8,128)(2,1)S(1)}, bf16[16,32,128]{2,1,0:T(8,128)(2,1)S(1)}, u32[]{:S(2)}, u32[]{:S(2)}) collective-permute-start(bf16[16,32,128]{2,1,0:T(8,128)(2,1)S(1)} %copy.77), channel_id=1, source_target_pairs={{0,508},{4,0},{8,4},{12,8},{16,12},{20,16},{24,20},{28,24},{32,28}... | collective-permute-start | bytes 393224 | tf_op jit(solution)/shard_map/while/body/eval_jaxpr/ppermute | solution.py:18
  143.8 10.8 %copy-start.1 = (f32[128,128]{1,0:T(8,128)}, f32[128,128]{1,0:T(8,128)S(1)}, u32[]{:S(2)}) copy-start(f32[128,128]{1,0:T(8,128)S(1)} %get-tuple-element.376) | copy-start | bytes 196612 | tf_op jit(solution)/shard_map/while
  143.8 16.0 %collective-permute-start = (bf16[16,32,128]{2,1,0:T(8,128)(2,1)S(1)}, bf16[16,32,128]{2,1,0:T(8,128)(2,1)S(1)}, u32[]{:S(2)}, u32[]{:S(2)}) collective-permute-start(bf16[16,32,128]{2,1,0:T(8,128)(2,1)S(1)} %copy.77), channel_id=1, source_target_pairs={{0,508},{4,0},{8,4},{12,8},{16,12},{20,16},{24,20},{28,24},{32,28}... | collective-permute-start | bytes 393224 | tf_op jit(solution)/shard_map/while/body/eval_jaxpr/ppermute | solution.py:18
  156.6 3.8 %copy-start.2 = (f32[128,128]{1,0:T(8,128)S(1)}, f32[128,128]{1,0:T(8,128)}, u32[]{:S(2)}) copy-start(f32[128,128]{1,0:T(8,128)} %copy-done.1) | copy-start | bytes 196612 | tf_op jit(solution)/shard_map/while
  160.4 10.9 %copy-start.1 = (f32[128,128]{1,0:T(8,128)}, f32[128,128]{1,0:T(8,128)S(1)}, u32[]{:S(2)}) copy-start(f32[128,128]{1,0:T(8,128)S(1)} %get-tuple-element.376) | copy-start | bytes 196612 | tf_op jit(solution)/shard_map/while
  160.4 16.2 %collective-permute-start = (bf16[16,32,128]{2,1,0:T(8,128)(2,1)S(1)}, bf16[16,32,128]{2,1,0:T(8,128)(2,1)S(1)}, u32[]{:S(2)}, u32[]{:S(2)}) collective-permute-start(bf16[16,32,128]{2,1,0:T(8,128)(2,1)S(1)} %copy.77), channel_id=1, source_target_pairs={{0,508},{4,0},{8,4},{12,8},{16,12},{20,16},{24,20},{28,24},{32,28}... | collective-permute-start | bytes 393224 | tf_op jit(solution)/shard_map/while/body/eval_jaxpr/ppermute | solution.py:18
  173.2 3.8 %copy-start.2 = (f32[128,128]{1,0:T(8,128)S(1)}, f32[128,128]{1,0:T(8,128)}, u32[]{:S(2)}) copy-start(f32[128,128]{1,0:T(8,128)} %copy-done.1) | copy-start | bytes 196612 | tf_op jit(solution)/shard_map/while
  (20 other events, 17.3 us)
Sparse Core Ops, SparseCore 0:
  185.2 55.4 reduce-scatter.1
